TPU v7x, 32 devices: a whole 2x2x4 slice. The times are simulated.
32 devices in a mesh: ctx: 16 (over z, y, x), tp: 2 (over core).
Axes of the slice: x: 2, y: 2, z: 4, core: 2. Of those that a mesh axis runs over, the one named last changes fastest.
Arguments:
- queries: bfloat16 [4096, 2048], P('tp', 'ctx'), may hold values from -6 to 6
- keys_in: bfloat16 [4096, 2048], P('tp', 'ctx'), may hold values from -6 to 6
- values_in: bfloat16 [4096, 2048], P('tp', 'ctx'), may hold values from -6 to 6
- grad_out: bfloat16 [4096, 2048], P('tp', 'ctx'), may hold values from -6 to 6
- residue: float32 [64, 16], replicated, may hold values from -0.07 to 0.07
- decay_rate: float32 [64, 16], replicated, may hold values from 9.765625e-05 to 0.0333333333
Outputs:
- grad_queries: bfloat16 [4096, 2048], P('tp', 'ctx')
- grad_keys: bfloat16 [4096, 2048], P('tp', 'ctx')
- grad_values: bfloat16 [4096, 2048], P('tp', 'ctx')
- grad_residue: float32 [64, 16], replicated
- grad_decay: float32 [64, 16], replicated
All inputs are finite; a program needn't handle non-finite values.
Results may differ from a plain program's by a relative error of at most 0.0085.
Values may be sent and summed in bfloat16 or wider, within the bound.
No kernel may reach another device: no remote copies, remote signals or barrier semaphores. Data moves between devices by JAX's collectives and lax.ppermute only.
A program may use at most 128 MiB of HBM per device.

v0:
```python
import math
import jax
import jax.numpy as jnp
from jax import lax
from jax.sharding import PartitionSpec as P


def dft_tables(size_a, size_b):
    total = size_a * size_b
    rows_a = jnp.arange(size_a, dtype=jnp.int32)
    rows_b = jnp.arange(size_b, dtype=jnp.int32)
    phase_a = (rows_a[:, None] * rows_a[None, :] % size_a).astype(jnp.float32) * (
        2.0 * math.pi / size_a
    )
    phase_b = (rows_b[:, None] * rows_b[None, :] % size_b).astype(jnp.float32) * (
        2.0 * math.pi / size_b
    )
    phase_turn = (rows_a[:, None] * rows_b[None, :] % total).astype(jnp.float32) * (
        2.0 * math.pi / total
    )
    fb_re = jnp.cos(phase_b)
    fb_im = -jnp.sin(phase_b)
    fa_pair = jnp.stack([jnp.cos(phase_a), -jnp.sin(phase_a)], axis=0)
    forward_b = jnp.stack([jnp.stack([fb_re, fb_im], 0), jnp.stack([-fb_im, fb_re], 0)], 0)
    inverse_b = jnp.stack([jnp.stack([fb_re, -fb_im], 0), jnp.stack([fb_im, fb_re], 0)], 0)
    return (fa_pair, forward_b, inverse_b, jnp.cos(phase_turn), -jnp.sin(phase_turn))


def forward_dft(signal, tables):
    fa_pair, forward_b, inverse_b, turn_re, turn_im = tables
    highest = lax.Precision.HIGHEST
    first = jnp.einsum("cab,pak->cpkb", signal, fa_pair, precision=highest)
    first_re = first[:, 0]
    first_im = first[:, 1]
    turned = jnp.stack(
        [
            first_re * turn_re[None] - first_im * turn_im[None],
            first_re * turn_im[None] + first_im * turn_re[None],
        ],
        axis=1,
    )
    return jnp.einsum("cpkb,pqbm->cqkm", turned, forward_b, precision=highest)


def inverse_real(spectrum, tables):
    fa_pair, forward_b, inverse_b, turn_re, turn_im = tables
    highest = lax.Precision.HIGHEST
    middle = jnp.einsum("cpkm,pqbm->cqkb", spectrum, inverse_b, precision=highest)
    middle_re = middle[:, 0]
    middle_im = middle[:, 1]
    back = jnp.stack(
        [
            middle_re * turn_re[None] + middle_im * turn_im[None],
            middle_im * turn_re[None] - middle_re * turn_im[None],
        ],
        axis=1,
    )
    result = jnp.einsum("cpkb,pak->cab", back, fa_pair, precision=highest)
    total = result.shape[1] * result.shape[2]
    return result.reshape(result.shape[0], total) / total


def spectral_work(gated, conv_grad, res_chan, dec_chan):
    chans, length = gated.shape
    total = 2 * length
    size_a = math.isqrt(total)
    while total % size_a != 0:
        size_a -= 1
    size_b = total // size_a
    tables = dft_tables(size_a, size_b)
    highest = lax.Precision.HIGHEST
    positions = jnp.arange(length).astype(jnp.float32)
    basis = jnp.exp(-dec_chan[:, :, None] * positions[None, None, :])
    filt = jnp.einsum("cm,cmt->ct", res_chan, basis, precision=highest)
    fields = jnp.concatenate(
        [gated.astype(jnp.float32), filt, conv_grad.astype(jnp.float32)], axis=0
    )
    padded = jnp.concatenate([fields, jnp.zeros((3 * chans, length), jnp.float32)], axis=1)
    spectra = forward_dft(padded.reshape(3 * chans, size_a, size_b), tables)
    gated_re = spectra[:chans, 0]
    gated_im = spectra[:chans, 1]
    filt_re = spectra[chans : 2 * chans, 0]
    filt_im = spectra[chans : 2 * chans, 1]
    cot_re = spectra[2 * chans :, 0]
    cot_im = spectra[2 * chans :, 1]
    products_re = jnp.concatenate(
        [
            gated_re * filt_re - gated_im * filt_im,
            filt_re * cot_re + filt_im * cot_im,
            gated_re * cot_re + gated_im * cot_im,
        ],
        axis=0,
    )
    products_im = jnp.concatenate(
        [
            gated_re * filt_im + gated_im * filt_re,
            filt_re * cot_im - filt_im * cot_re,
            gated_re * cot_im - gated_im * cot_re,
        ],
        axis=0,
    )
    results = inverse_real(jnp.stack([products_re, products_im], axis=1), tables)[:, :length]
    conv = results[:chans].astype(jnp.bfloat16)
    input_grad = results[chans : 2 * chans].astype(jnp.bfloat16)
    filter_grad = results[2 * chans :]
    res_terms = jnp.einsum("ct,cmt->cm", filter_grad, basis, precision=highest)
    dec_terms = (
        -res_chan
        * dec_chan
        * jnp.einsum("ct,cmt->cm", filter_grad * positions[None, :], basis, precision=highest)
    )
    return (conv, input_grad, res_terms, dec_terms)


def product_bf(first, second):
    return (first.astype(jnp.float32) * second.astype(jnp.float32)).astype(jnp.bfloat16)


def per_device(queries, keys_in, values_in, grad_out, residue, decay_rate):
    chans_tp, tokens_dev = queries.shape
    ctx_count = lax.axis_size("ctx")
    groups_count = residue.shape[0]
    highest = lax.Precision.HIGHEST
    chans_dev = chans_tp // ctx_count
    channel_ids = (
        lax.axis_index("tp") * chans_tp
        + lax.axis_index("ctx") * chans_dev
        + jnp.arange(chans_dev, dtype=jnp.int32)
    )
    onehot = (
        (channel_ids % groups_count)[:, None] == jnp.arange(groups_count, dtype=jnp.int32)[None, :]
    ).astype(jnp.float32)
    res_chan = jnp.dot(onehot, residue, precision=highest)
    dec_chan = jnp.dot(onehot, decay_rate, precision=highest)

    def to_blocks(field):
        return field.reshape(ctx_count, chans_dev, tokens_dev)

    def to_whole(field):
        return field.reshape(chans_dev, ctx_count * tokens_dev)

    def to_return(field):
        return field.reshape(1, chans_dev, ctx_count * tokens_dev)

    moved_query, moved_key, moved_value, moved_grad = (
        lax.all_to_all(to_blocks(queries), "ctx", split_axis=0, concat_axis=2, tiled=True),
        lax.all_to_all(to_blocks(keys_in), "ctx", split_axis=0, concat_axis=2, tiled=True),
        lax.all_to_all(to_blocks(values_in), "ctx", split_axis=0, concat_axis=2, tiled=True),
        lax.all_to_all(to_blocks(grad_out), "ctx", split_axis=0, concat_axis=2, tiled=True),
    )
    whole_query = to_whole(moved_query)
    whole_key = to_whole(moved_key)
    whole_value = to_whole(moved_value)
    whole_grad = to_whole(moved_grad)
    gated = product_bf(whole_key, whole_value)
    conv_grad = product_bf(whole_grad, whole_query)
    conv, input_grad, res_terms, dec_terms = spectral_work(gated, conv_grad, res_chan, dec_chan)
    grad_q_ch = product_bf(whole_grad, conv)
    grad_k_ch = product_bf(input_grad, whole_value)
    grad_v_ch = product_bf(input_grad, whole_key)
    back_q, back_k, back_v = (
        lax.all_to_all(to_return(grad_q_ch), "ctx", split_axis=2, concat_axis=0, tiled=True),
        lax.all_to_all(to_return(grad_k_ch), "ctx", split_axis=2, concat_axis=0, tiled=True),
        lax.all_to_all(to_return(grad_v_ch), "ctx", split_axis=2, concat_axis=0, tiled=True),
    )
    grad_queries = back_q.reshape(chans_tp, tokens_dev)
    grad_keys = back_k.reshape(chans_tp, tokens_dev)
    grad_values = back_v.reshape(chans_tp, tokens_dev)
    res_group = jnp.dot(onehot.T, res_terms, precision=highest)
    dec_group = jnp.dot(onehot.T, dec_terms, precision=highest)
    res_total, dec_total = lax.psum((res_group, dec_group), ("ctx", "tp"))
    whole_length = ctx_count * tokens_dev
    return (
        grad_queries,
        grad_keys,
        grad_values,
        res_total / whole_length,
        dec_total / whole_length,
    )


def solution(mesh):
    in_specs = (P("tp", "ctx"), P("tp", "ctx"), P("tp", "ctx"), P("tp", "ctx"), P(), P())
    out_specs = (P("tp", "ctx"), P("tp", "ctx"), P("tp", "ctx"), P(), P())
    return jax.shard_map(
        per_device, mesh=mesh, in_specs=in_specs, out_specs=out_specs, check_vma=False
    )
```

profile of v0, /device:TPU:0, one launch (start us, length us, event | category | flops | bytes accessed | tf_op | source)
XLA Modules:
  0.0 373.3 jit_solution(8923494113238331859)
XLA Ops:
  0.6 23.4 %all_to_all.81 = bf16[16,128,128]{2,1,0:T(8,128)(2,1)S(1)} all-to-all(bf16[16,128,128]{2,1,0:T(8,128)(2,1)} %bitcast.183), channel_id=1, replica_groups=mesh['ctx'=16,'tp'=2] {'ctx'}, dimensions={0} | all-to-all | bytes 1048576 | tf_op jit(solution)/shard_map/all_to_all | solution.py:147
  24.1 3.9 %all-to-all-start.2 = ((bf16[16,128,128]{2,1,0:T(8,128)(2,1)}), bf16[16,128,128]{2,1,0:T(8,128)(2,1)S(1)}, u32[]{:S(2)}, u32[]{:S(2)}) async-start(bf16[16,128,128]{2,1,0:T(8,128)(2,1)} %bitcast.184), calls=%async_computation.2 | async-start | bytes 1048576 | tf_op jit(solution)/shard_map/all_to_all | solution.py:148
  29.1 13.3 %all-to-all-done.2 = bf16[16,128,128]{2,1,0:T(8,128)(2,1)S(1)} async-done(((bf16[16,128,128]{2,1,0:T(8,128)(2,1)}), bf16[16,128,128]{2,1,0:T(8,128)(2,1)S(1)}, u32[]{:S(2)}, u32[]{:S(2)}) %all-to-all-start.2) | async-done | bytes 524320 | tf_op jit(solution)/shard_map/all_to_all | solution.py:148
  42.5 3.9 %all-to-all-start.3 = ((bf16[16,128,128]{2,1,0:T(8,128)(2,1)}), bf16[16,128,128]{2,1,0:T(8,128)(2,1)S(1)}, u32[]{:S(2)}, u32[]{:S(2)}) async-start(bf16[16,128,128]{2,1,0:T(8,128)(2,1)} %bitcast.185), calls=%async_computation.3 | async-start | bytes 1048576 | tf_op jit(solution)/shard_map/all_to_all | solution.py:146
  47.3 5.1 %multiply_reduce_fusion.1 = f32[128,2048]{1,0:T(8,128)S(1)} fusion(f32[128,16]{1,0:T(8,128)S(1)} %copy.93, f32[2048]{0:T(1024)S(1)} %iota_convert_fusion, f32[128,16]{1,0:T(8,128)S(1)} %copy.49), kind=kLoop, calls=%fused_computation.1 | loop fusion | flops 12320768 | bytes 1073152
  52.5 1.3 copy.69
  54.1 6.6 %all-to-all-done.3 = bf16[16,128,128]{2,1,0:T(8,128)(2,1)S(1)} async-done(((bf16[16,128,128]{2,1,0:T(8,128)(2,1)}), bf16[16,128,128]{2,1,0:T(8,128)(2,1)S(1)}, u32[]{:S(2)}, u32[]{:S(2)}) %all-to-all-start.3) | async-done | bytes 524320 | tf_op jit(solution)/shard_map/all_to_all | solution.py:146
  60.8 4.4 %all-to-all-start = ((bf16[16,128,128]{2,1,0:T(8,128)(2,1)}), bf16[16,128,128]{2,1,0:T(8,128)(2,1)}, u32[]{:S(2)}, u32[]{:S(2)}) async-start(bf16[16,128,128]{2,1,0:T(8,128)(2,1)} %bitcast.1), calls=%async_computation | async-start | bytes 1048576 | tf_op jit(solution)/shard_map/all_to_all | solution.py:149
  65.8 1.5 convert_bitcast_fusion.1
  67.7 1.5 convert_bitcast_fusion
  69.2 1.3 copy.50
  70.5 8.6 %all-to-all-done = bf16[16,128,128]{2,1,0:T(8,128)(2,1)} async-done(((bf16[16,128,128]{2,1,0:T(8,128)(2,1)}), bf16[16,128,128]{2,1,0:T(8,128)(2,1)}, u32[]{:S(2)}, u32[]{:S(2)}) %all-to-all-start) | async-done | bytes 524320 | tf_op jit(solution)/shard_map/all_to_all | solution.py:149
  79.1 2.1 convert_bitcast_fusion.3
  81.3 1.6 copy.46
  82.8 2.0 fusion.33
  85.3 14.2 %fusion.17 = f32[384,2,64,64]{0,2,3,1:T(8,128)S(1)} fusion(f32[384,64,64]{0,2,1:T(8,128)S(1)} %bitcast.170, f32[1,64,64]{1,2,0:T(8,128)S(1)} %get-tuple-element.32, f32[1,64,64]{1,2,0:T(8,128)S(1)} %get-tuple-element.33), kind=kOutput, calls=%fused_computation.33 | convolution fusion | flops 2415927296 | bytes 18907136 | tf_op jit(solution)/shard_map/cab,pak->cpkb/dot_general | solution.py:32
  99.5 3.7 multiply_subtract_fusion.1
  103.3 9.6 %pad_maximum_fusion = f32[384,2,64,64]{0,2,3,1:T(8,128)} fusion(f32[384,1,64,64]{0,2,3,1:T(8,128)} %get-tuple-element.10, f32[384,1,64,64]{0,2,3,1:T(8,128)S(1)} %get-tuple-element.9), kind=kLoop, calls=%fused_computation.4 | loop fusion | flops 3145728 | bytes 25165824 | tf_op jit(solution)/shard_map/stack | solution.py:35
  112.9 22.9 %fusion.20 = f32[384,2,64,64]{0,3,2,1:T(8,128)S(1)} fusion(f32[384,2,64,64]{0,2,3,1:T(8,128)} %pad_maximum_fusion, f32[1,2,64,64]{2,3,1,0:T(8,128)S(1)} %get-tuple-element.23, f32[1,2,64,64]{2,3,1,0:T(8,128)S(1)} %get-tuple-element.26), kind=kOutput, calls=%fused_computation.34 | convolution fusion | flops 4831854592 | bytes 25231360 | tf_op jit(solution)/shard_map/cpkb,pqbm->cqkm/dot_general | solution.py:42
  135.7 2.8 subtract_bitcast_fusion.1
  138.5 4.3 %subtract_bitcast_fusion.2 = (f32[128,64,64]{0,2,1:T(8,128)}, f32[128,64,64]{0,2,1:T(8,128)}, f32[128,64,64]{0,2,1:T(8,128)}, f32[128,64,64]{0,2,1:T(8,128)}) fusion(f32[384,2,64,64]{0,3,2,1:T(8,128)S(1)} %fusion.20), kind=kLoop, calls=%fused_computation.41 | loop fusion | flops 6291456 | bytes 20971520 | tf_op jit(solution)/shard_map/sub | solution.py:88
  142.8 3.7 maximum_bitcast_fusion.1
  148.2 13.7 %fusion.23 = f32[2,64,384,64]{2,1,3,0:T(8,128)} fusion(f32[384,1,64,64]{0,3,2,1:T(8,128)S(1)} %maximum_bitcast_fusion.1, f32[384,1,64,64]{0,3,2,1:T(8,128)S(1)} %maximum_bitcast_fusion, f32[1,2,64,64]{2,3,1,0:T(8,128)S(1)} %get-tuple-element.27, f32[1,2,64,64]{2,3,1,0:T(8,128)S(1)} %get-tuple-element.22), kind=kOutput, calls=%fused_computation.35 | convolution fusion | flops 4835000320 | bytes 25231360 | tf_op jit(solution)/shard_map/cpkm,pqbm->cqkb/dot_general | solution.py:48
  161.9 16.4 %copy.121 = f32[2,64,384,64]{2,3,1,0:T(8,128)} copy(f32[2,64,384,64]{2,1,3,0:T(8,128)} %fusion.23) | data formatting | bytes 25165824 | tf_op jit(solution)/shard_map/cpkm,pqbm->cqkb/dot_general | solution.py:48
  178.3 6.0 %multiply_add_fusion = (f32[384,1,64,64]{0,2,3,1:T(8,128)S(1)}, f32[384,1,64,64]{0,2,3,1:T(8,128)S(1)}) fusion(f32[384,2,64,64]{0,2,3,1:T(8,128)} %bitcast.168, f32[64,64]{0,1:T(8,128)S(1)} %get-tuple-element.34, f32[64,64]{0,1:T(8,128)S(1)} %get-tuple-element.35), kind=kLoop, calls=%fused_computation.30 | loop fusion | flops 9437184 | bytes 25198592 | tf_op jit(solution)/shard_map/add | solution.py:53
  184.3 7.4 %fusion.13 = f32[384,64,64]{0,1,2:T(8,128)S(1)} fusion(f32[384,1,64,64]{0,2,3,1:T(8,128)S(1)} %get-tuple-element.8, f32[384,1,64,64]{0,2,3,1:T(8,128)S(1)} %get-tuple-element.7, f32[1,64,64]{1,2,0:T(8,128)S(1)} %get-tuple-element.32, f32[1,64,64]{1,2,0:T(8,128)S(1)} %get-tuple-element.33), kind=kOutput, calls=%fused_computation.23 | convolution fusion | flops 2420645888 | bytes 18907136 | tf_op jit(solution)/shard_map/cpkb,pak->cab/dot_general | solution.py:58
  191.7 3.6 copy.59
  196.2 1.2 copy-done.4
  197.4 1.1 copy-done.6
  198.5 1.0 copy-done.8
  199.8 8.5 %copy.124 = bf16[1,128,2048]{1,0,2:T(2,128)(2,1)S(1)} copy(bf16[1,128,2048]{1,2,0:T(8,128)(2,1)S(1)} %bitcast.182) | data formatting | bytes 1048576 | tf_op jit(solution)/shard_map/reshape | solution.py:143
  208.9 11.5 %reduce.4 = bf16[2048,128]{1,0:T(8,128)(2,1)S(1)} reduce(bf16[2048,1,128]{2,1,0:T(2,128)(2,1)S(1)} %bitcast.174, bf16[]{:T(256)} %broadcast.254), dimensions={1}, to_apply=%bitcast.167.reduce_sub_computation | reduce | bytes 1048578
  221.3 4.0 %all-to-all-start.4 = ((bf16[16,2,8192]{2,1,0:T(2,128)(2,1)}), bf16[16,2,8192]{2,1,0:T(2,128)(2,1)S(1)}, u32[]{:S(2)}, u32[]{:S(2)}) async-start(bf16[16,2,8192]{2,1,0:T(2,128)(2,1)} %reshape.263), calls=%async_computation.4 | async-start | bytes 1048576 | tf_op jit(solution)/shard_map/all_to_all | solution.py:162
  225.3 8.1 %copy.123 = bf16[1,128,2048]{1,0,2:T(2,128)(2,1)S(1)} copy(bf16[1,128,2048]{1,2,0:T(8,128)(2,1)S(1)} %bitcast.181) | data formatting | bytes 1048576 | tf_op jit(solution)/shard_map/reshape | solution.py:143
  233.5 11.5 %reduce.5 = bf16[2048,128]{1,0:T(8,128)(2,1)S(1)} reduce(bf16[2048,1,128]{2,1,0:T(2,128)(2,1)S(1)} %bitcast.176, bf16[]{:T(256)} %broadcast.254), dimensions={1}, to_apply=%bitcast.166.reduce_sub_computation | reduce | bytes 1048578
  245.9 8.3 %copy.122 = bf16[1,128,2048]{1,0,2:T(2,128)(2,1)S(1)} copy(bf16[1,128,2048]{1,2,0:T(8,128)(2,1)S(1)} %bitcast.180) | data formatting | bytes 1048576 | tf_op jit(solution)/shard_map/reshape | solution.py:143
  254.2 11.5 %reduce.6 = bf16[2048,128]{1,0:T(8,128)(2,1)S(1)} reduce(bf16[2048,1,128]{2,1,0:T(2,128)(2,1)S(1)} %bitcast.175, bf16[]{:T(256)} %broadcast.254), dimensions={1}, to_apply=%bitcast.165.reduce_sub_computation | reduce | bytes 1048578
  266.7 7.0 %all-to-all-start.5 = ((bf16[16,2,8192]{2,1,0:T(2,128)(2,1)}), bf16[16,2,8192]{2,1,0:T(2,128)(2,1)S(1)}, u32[]{:S(2)}, u32[]{:S(2)}) async-start(bf16[16,2,8192]{2,1,0:T(2,128)(2,1)} %reshape.265), calls=%async_computation.5 | async-start | bytes 1048576 | tf_op jit(solution)/shard_map/all_to_all | solution.py:163
  273.7 1.6 slice_multiply_fusion
  275.3 2.0 copy.77
  277.6 3.3 multiply_reduce_fusion
  280.9 6.4 %all-to-all-done.5 = bf16[16,2,8192]{2,1,0:T(2,128)(2,1)S(1)} async-done(((bf16[16,2,8192]{2,1,0:T(2,128)(2,1)}), bf16[16,2,8192]{2,1,0:T(2,128)(2,1)S(1)}, u32[]{:S(2)}, u32[]{:S(2)}) %all-to-all-start.5) | async-done | bytes 524320 | tf_op jit(solution)/shard_map/all_to_all | solution.py:163
  287.3 3.8 %all-to-all-start.6 = ((bf16[16,2,8192]{2,1,0:T(2,128)(2,1)}), bf16[16,2,8192]{2,1,0:T(2,128)(2,1)S(1)}, u32[]{:S(2)}, u32[]{:S(2)}) async-start(bf16[16,2,8192]{2,1,0:T(2,128)(2,1)} %reshape.267), calls=%async_computation.6 | async-start | bytes 1048576 | tf_op jit(solution)/shard_map/all_to_all | solution.py:164
  291.2 34.5 %fusion = f32[128,1,16]{2,1,0:T(1,128)S(1)} fusion(f32[128,2048,1]{1,2,0:T(1,128)S(1)} %copy-done.15, f32[2048]{0:T(1024)S(1)} %iota_convert_fusion, f32[128,16]{1,0:T(8,128)S(1)} %copy-done.17), kind=kOutput, calls=%fused_computation.3 | convolution fusion | flops 54525952 | bytes 1073152 | tf_op jit(solution)/shard_map/ct,cmt->cm/dot_general | solution.py:106
  326.3 40.7 %all-reduce.1 = (f32[64,16]{0,1:T(8,128)S(1)}, f32[64,16]{0,1:T(8,128)S(1)}) all-reduce(f32[64,16]{0,1:T(8,128)S(1)} %fusion.43, f32[64,16]{0,1:T(8,128)S(1)} %fusion.42), channel_id=1, replica_groups=mesh['ctx'=16,'tp'=2] {'ctx','tp'}, use_global_device_ids=true, to_apply=%region_0.1 | all-reduce | flops 2048 | bytes 16384 | tf_op jit(solution)/shard_map/psum | solution.py:171
  368.8 1.0 copy.61
  370.4 1.0 copy.63
  372.1 1.0 copy.65
  (74 shorter events, 13.6 us)
Async XLA Ops:
  0.6 45.7 %copy-start = (f32[64,16]{0,1:T(8,128)S(1)}, f32[64,16]{0,1:T(8,128)}, u32[]{:S(2)}) copy-start(f32[64,16]{0,1:T(8,128)} %param.11) | copy-start | bytes 12292
  24.1 18.4 %all-to-all-start.2 = ((bf16[16,128,128]{2,1,0:T(8,128)(2,1)}), bf16[16,128,128]{2,1,0:T(8,128)(2,1)S(1)}, u32[]{:S(2)}, u32[]{:S(2)}) async-start(bf16[16,128,128]{2,1,0:T(8,128)(2,1)} %bitcast.184), calls=%async_computation.2 | async-start | bytes 1048576 | tf_op jit(solution)/shard_map/all_to_all | solution.py:148
  28.1 37.3 %copy-start.18 = (s32[128]{0:T(128)}, s32[128]{0:T(128)S(1)}, u32[]{:S(2)}) copy-start(s32[128]{0:T(128)S(1)} %and_select_fusion) | copy-start | bytes 1540
  42.5 22.9 %copy-start.13 = (bf16[16,128,128]{2,1,0:T(8,128)(2,1)}, bf16[16,128,128]{2,1,0:T(8,128)(2,1)S(1)}, u32[]{:S(2)}) copy-start(bf16[16,128,128]{2,1,0:T(8,128)(2,1)S(1)} %all-to-all-done.2) | copy-start | bytes 1572868
  42.5 18.3 %all-to-all-start.3 = ((bf16[16,128,128]{2,1,0:T(8,128)(2,1)}), bf16[16,128,128]{2,1,0:T(8,128)(2,1)S(1)}, u32[]{:S(2)}, u32[]{:S(2)}) async-start(bf16[16,128,128]{2,1,0:T(8,128)(2,1)} %bitcast.185), calls=%async_computation.3 | async-start | bytes 1048576 | tf_op jit(solution)/shard_map/all_to_all | solution.py:146
  47.3 18.2 %copy-start.16 = (f32[128,16]{1,0:T(8,128)}, f32[128,16]{1,0:T(8,128)S(1)}, u32[]{:S(2)}) copy-start(f32[128,16]{1,0:T(8,128)S(1)} %copy.49) | copy-start | bytes 24580
  60.8 4.6 %copy-start.14 = (bf16[16,128,128]{2,1,0:T(8,128)(2,1)}, bf16[16,128,128]{2,1,0:T(8,128)(2,1)S(1)}, u32[]{:S(2)}) copy-start(bf16[16,128,128]{2,1,0:T(8,128)(2,1)S(1)} %all-to-all-done.3) | copy-start | bytes 1572868
  60.8 18.4 %all-to-all-start = ((bf16[16,128,128]{2,1,0:T(8,128)(2,1)}), bf16[16,128,128]{2,1,0:T(8,128)(2,1)}, u32[]{:S(2)}, u32[]{:S(2)}) async-start(bf16[16,128,128]{2,1,0:T(8,128)(2,1)} %bitcast.1), calls=%async_computation | async-start | bytes 1048576 | tf_op jit(solution)/shard_map/all_to_all | solution.py:149
  65.8 19.0 %copy-start.3 = (f32[1,128,16,128]{1,3,2,0:T(8,128)}, f32[1,128,16,128]{1,3,2,0:T(8,128)S(1)}, u32[]{:S(2)}) copy-start(f32[1,128,16,128]{1,3,2,0:T(8,128)S(1)} %copy.47) | copy-start | bytes 3145732
  67.7 17.2 %copy-start.5 = (f32[1,128,16,128]{1,3,2,0:T(8,128)}, f32[1,128,16,128]{1,3,2,0:T(8,128)S(1)}, u32[]{:S(2)}) copy-start(f32[1,128,16,128]{1,3,2,0:T(8,128)S(1)} %copy.48) | copy-start | bytes 3145732
  82.8 2.5 copy-start.7
  82.8 2.1 copy-start.12
  142.8 3.7 copy-start.9
  142.8 4.1 %copy-start.10 = (f32[128,64,64]{0,2,1:T(8,128)S(1)}, f32[128,64,64]{0,2,1:T(8,128)}, u32[]{:S(2)}) copy-start(f32[128,64,64]{0,2,1:T(8,128)} %get-tuple-element.12) | copy-start | bytes 6291460
  142.8 4.7 %copy-start.11 = (f32[128,64,64]{0,2,1:T(8,128)S(1)}, f32[128,64,64]{0,2,1:T(8,128)}, u32[]{:S(2)}) copy-start(f32[128,64,64]{0,2,1:T(8,128)} %get-tuple-element.13) | copy-start | bytes 6291460
  195.4 4.4 %copy-start.2 = (f32[384,64,64]{0,2,1:T(8,128)}, f32[384,64,64]{0,2,1:T(8,128)S(1)}, u32[]{:S(2)}) copy-start(f32[384,64,64]{0,2,1:T(8,128)S(1)} %copy.59) | copy-start | bytes 18874372
  195.4 2.0 copy-start.4
  195.4 3.1 copy-start.6
  195.4 4.1 %copy-start.8 = (f32[1,128,16,128]{1,3,2,0:T(8,128)S(1)}, f32[1,128,16,128]{1,3,2,0:T(8,128)}, u32[]{:S(2)}) copy-start(f32[1,128,16,128]{1,3,2,0:T(8,128)} %copy-done.7) | copy-start | bytes 3145732
  221.3 45.4 %all-to-all-start.4 = ((bf16[16,2,8192]{2,1,0:T(2,128)(2,1)}), bf16[16,2,8192]{2,1,0:T(2,128)(2,1)S(1)}, u32[]{:S(2)}, u32[]{:S(2)}) async-start(bf16[16,2,8192]{2,1,0:T(2,128)(2,1)} %reshape.263), calls=%async_computation.4 | async-start | bytes 1048576 | tf_op jit(solution)/shard_map/all_to_all | solution.py:162
  245.9 31.7 %copy-start.17 = (f32[128,16]{1,0:T(8,128)S(1)}, f32[128,16]{1,0:T(8,128)}, u32[]{:S(2)}) copy-start(f32[128,16]{1,0:T(8,128)} %copy-done.16) | copy-start | bytes 24580
  266.7 20.6 %all-to-all-start.5 = ((bf16[16,2,8192]{2,1,0:T(2,128)(2,1)}), bf16[16,2,8192]{2,1,0:T(2,128)(2,1)S(1)}, u32[]{:S(2)}, u32[]{:S(2)}) async-start(bf16[16,2,8192]{2,1,0:T(2,128)(2,1)} %reshape.265), calls=%async_computation.5 | async-start | bytes 1048576 | tf_op jit(solution)/shard_map/all_to_all | solution.py:163
  277.6 13.6 %copy-start.15 = (f32[128,2048,1]{1,2,0:T(1,128)S(1)}, f32[128,2048,1]{1,2,0:T(1,128)}, u32[]{:S(2)}) copy-start(f32[128,2048,1]{1,2,0:T(1,128)} %copy.77) | copy-start | bytes 3145732
  287.3 84.2 %all-to-all-start.6 = ((bf16[16,2,8192]{2,1,0:T(2,128)(2,1)}), bf16[16,2,8192]{2,1,0:T(2,128)(2,1)S(1)}, u32[]{:S(2)}, u32[]{:S(2)}) async-start(bf16[16,2,8192]{2,1,0:T(2,128)(2,1)} %reshape.267), calls=%async_computation.6 | async-start | bytes 1048576 | tf_op jit(solution)/shard_map/all_to_all | solution.py:164
  291.2 34.6 %copy-start.19 = (s32[128]{0:T(128)S(1)}, s32[128]{0:T(128)}, u32[]{:S(2)}) copy-start(s32[128]{0:T(128)} %copy-done.18) | copy-start | bytes 1540
  291.2 34.6 %copy-start.20 = (f32[128,16]{0,1:T(8,128)S(1)}, f32[128,16]{0,1:T(8,128)}, u32[]{:S(2)}) copy-start(f32[128,16]{0,1:T(8,128)} %get-tuple-element.29) | copy-start | bytes 24580
  367.6 5.5 %copy-start.1 = (f32[64,16]{0,1:T(8,128)S(1)}, f32[64,16]{0,1:T(8,128)}, u32[]{:S(2)}) copy-start(f32[64,16]{0,1:T(8,128)} %param.11) | copy-start | bytes 12292
where the time goes:
time: 377 us; the launch traced here: 373 us
  matrix products  95 us (25%)
  other arithmetic  85.7 us (23%)
  local copies, waits for them, and re-layouts  65 us (17%)
  blocking collectives  64.1 us (17%)
  waiting for transfers between devices  35 us (9%)
  starting transfers between devices  27.1 us (7%)
    unnamed x5, other arithmetic  43 us
    psum x1, blocking collectives, per_device(): res_total, dec_total = lax.psum((res_group, dec_group), ('ctx', 'tp'))  40.7 us
    dot_general x1, matrix products, spectral_work(): res_terms = jnp.einsum('ct,cmt->cm', filter_grad, basis, precision=highest)  34.5 us
    reshape x3, local copies, waits for them, and re-layouts, to_return(): return field.reshape(1, chans_dev, ctx_count * tokens_dev)  25 us
    all_to_all x1, blocking collectives, per_device(): lax.all_to_all(to_blocks(keys_in), 'ctx', split_axis=0, concat_axis=2, ti...  23.4 us
    dot_general x1, matrix products, forward_dft(): return jnp.einsum('cpkb,pqbm->cqkm', turned, forward_b, precision=highest)  22.9 us
    dot_general x1, local copies, waits for them, and re-layouts, inverse_real(): jnp.einsum('cpkm,pqbm->cqkb', spectrum, inverse_b, precision=highest)  16.4 us
    dot_general x1, matrix products, forward_dft(): first = jnp.einsum('cab,pak->cpkb', signal, fa_pair, precision=highest)  14.2 us
  transfers between devices with their start and end apart: 6, of which 4 were waited for; matrix products, arithmetic and copies ran while one was open for 27% of the time, Pallas kernels for 0%

commit v1 on v0

--- a/solution.py
+++ b/solution.py
@@ -3,6 +3,10 @@
 import jax.numpy as jnp
 from jax import lax
 from jax.sharding import PartitionSpec as P
+
+
+def number_array_in(chunk):
+    return lax.psum(lax.psum(chunk, "tp"), "ctx")
 
 
 def dft_tables(size_a, size_b):
@@ -168,7 +172,7 @@
     grad_values = back_v.reshape(chans_tp, tokens_dev)
     res_group = jnp.dot(onehot.T, res_terms, precision=highest)
     dec_group = jnp.dot(onehot.T, dec_terms, precision=highest)
-    res_total, dec_total = lax.psum((res_group, dec_group), ("ctx", "tp"))
+    res_total, dec_total = number_array_in((res_group, dec_group))
     whole_length = ctx_count * tokens_dev
     return (
         grad_queries,

time: 377 us -> 417 us (1.11)
  blocking collectives: 64.1 us -> 104 us
    psum x1 -> x2, blocking collectives: 40.7 us -> 80.4 us  [number_array_in(): return lax.psum(lax.psum(chunk, 'tp'), 'ctx')]
  transfers between devices with their start and end apart: 6 -> 6, of which waited for: 4 -> 4; matrix products, arithmetic and copies ran while one was open for 27% -> 25% of each run, Pallas kernels for 0% -> 0%
where the time goes in v1:
time: 417 us; the launch traced here: 413 us
  blocking collectives  104 us (25%)
  matrix products  95.1 us (23%)
  other arithmetic  85.7 us (21%)
  local copies, waits for them, and re-layouts  65 us (16%)
  waiting for transfers between devices  35 us (8%)
  starting transfers between devices  27.1 us (6%)
    psum x2, blocking collectives, number_array_in(): return lax.psum(lax.psum(chunk, 'tp'), 'ctx')  80.4 us
    unnamed x5, other arithmetic  43 us
    dot_general x1, matrix products, spectral_work(): res_terms = jnp.einsum('ct,cmt->cm', filter_grad, basis, precision=highest)  34.5 us
    reshape x3, local copies, waits for them, and re-layouts, to_return(): return field.reshape(1, chans_dev, ctx_count * tokens_dev)  25 us
    all_to_all x1, blocking collectives, per_device(): lax.all_to_all(to_blocks(keys_in), 'ctx', split_axis=0, concat_axis=2, ti...  23.4 us
    dot_general x1, matrix products, forward_dft(): return jnp.einsum('cpkb,pqbm->cqkm', turned, forward_b, precision=highest)  22.9 us
    dot_general x1, local copies, waits for them, and re-layouts, inverse_real(): jnp.einsum('cpkm,pqbm->cqkb', spectrum, inverse_b, precision=highest)  16.4 us
    dot_general x1, matrix products, forward_dft(): first = jnp.einsum('cab,pak->cpkb', signal, fa_pair, precision=highest)  14.2 us
  transfers between devices with their start and end apart: 6, of which 4 were waited for; matrix products, arithmetic and copies ran while one was open for 25% of the time, Pallas kernels for 0%

profile of v1, /device:TPU:0, one launch (start us, length us, event | category | flops | bytes accessed | tf_op | source)
XLA Modules:
  0.0 413.1 jit_solution(1348056130374348260)
XLA Ops:
  0.6 23.4 %all_to_all.81 = bf16[16,128,128]{2,1,0:T(8,128)(2,1)S(1)} all-to-all(bf16[16,128,128]{2,1,0:T(8,128)(2,1)} %bitcast.183), channel_id=1, replica_groups=mesh['ctx'=16,'tp'=2] {'ctx'}, dimensions={0} | all-to-all | bytes 1048576 | tf_op jit(solution)/shard_map/all_to_all | solution.py:151
  24.1 3.9 all-to-all-start.2
  29.1 13.3 %all-to-all-done.2 = bf16[16,128,128]{2,1,0:T(8,128)(2,1)S(1)} async-done(((bf16[16,128,128]{2,1,0:T(8,128)(2,1)}), bf16[16,128,128]{2,1,0:T(8,128)(2,1)S(1)}, u32[]{:S(2)}, u32[]{:S(2)}) %all-to-all-start.2) | async-done | bytes 524320 | tf_op jit(solution)/shard_map/all_to_all | solution.py:152
  42.5 3.9 all-to-all-start.3
  47.3 5.1 %multiply_reduce_fusion.1 = f32[128,2048]{1,0:T(8,128)S(1)} fusion(f32[128,16]{1,0:T(8,128)S(1)} %copy.93, f32[2048]{0:T(1024)S(1)} %iota_convert_fusion, f32[128,16]{1,0:T(8,128)S(1)} %copy.49), kind=kLoop, calls=%fused_computation.1 | loop fusion | flops 12320768 | bytes 1073152
  52.5 1.3 copy.69
  54.1 6.6 %all-to-all-done.3 = bf16[16,128,128]{2,1,0:T(8,128)(2,1)S(1)} async-done(((bf16[16,128,128]{2,1,0:T(8,128)(2,1)}), bf16[16,128,128]{2,1,0:T(8,128)(2,1)S(1)}, u32[]{:S(2)}, u32[]{:S(2)}) %all-to-all-start.3) | async-done | bytes 524320 | tf_op jit(solution)/shard_map/all_to_all | solution.py:150
  60.8 4.4 %all-to-all-start = ((bf16[16,128,128]{2,1,0:T(8,128)(2,1)}), bf16[16,128,128]{2,1,0:T(8,128)(2,1)}, u32[]{:S(2)}, u32[]{:S(2)}) async-start(bf16[16,128,128]{2,1,0:T(8,128)(2,1)} %bitcast.1), calls=%async_computation | async-start | bytes 1048576 | tf_op jit(solution)/shard_map/all_to_all | solution.py:153
  65.8 1.5 convert_bitcast_fusion.1
  67.7 1.5 convert_bitcast_fusion
  69.2 1.3 copy.50
  70.5 8.6 %all-to-all-done = bf16[16,128,128]{2,1,0:T(8,128)(2,1)} async-done(((bf16[16,128,128]{2,1,0:T(8,128)(2,1)}), bf16[16,128,128]{2,1,0:T(8,128)(2,1)}, u32[]{:S(2)}, u32[]{:S(2)}) %all-to-all-start) | async-done | bytes 524320 | tf_op jit(solution)/shard_map/all_to_all | solution.py:153
  79.1 2.1 convert_bitcast_fusion.3
  81.3 1.6 copy.46
  82.8 2.0 fusion.33
  85.3 14.2 %fusion.17 = f32[384,2,64,64]{0,2,3,1:T(8,128)S(1)} fusion(f32[384,64,64]{0,2,1:T(8,128)S(1)} %bitcast.170, f32[1,64,64]{1,2,0:T(8,128)S(1)} %get-tuple-element.34, f32[1,64,64]{1,2,0:T(8,128)S(1)} %get-tuple-element.35), kind=kOutput, calls=%fused_computation.33 | convolution fusion | flops 2415927296 | bytes 18907136 | tf_op jit(solution)/shard_map/cab,pak->cpkb/dot_general | solution.py:36
  99.5 3.7 multiply_subtract_fusion.1
  103.3 9.6 %pad_maximum_fusion = f32[384,2,64,64]{0,2,3,1:T(8,128)} fusion(f32[384,1,64,64]{0,2,3,1:T(8,128)} %get-tuple-element.12, f32[384,1,64,64]{0,2,3,1:T(8,128)S(1)} %get-tuple-element.11), kind=kLoop, calls=%fused_computation.4 | loop fusion | flops 3145728 | bytes 25165824 | tf_op jit(solution)/shard_map/stack | solution.py:39
  112.9 22.9 %fusion.20 = f32[384,2,64,64]{0,3,2,1:T(8,128)S(1)} fusion(f32[384,2,64,64]{0,2,3,1:T(8,128)} %pad_maximum_fusion, f32[1,2,64,64]{2,3,1,0:T(8,128)S(1)} %get-tuple-element.25, f32[1,2,64,64]{2,3,1,0:T(8,128)S(1)} %get-tuple-element.28), kind=kOutput, calls=%fused_computation.34 | convolution fusion | flops 4831854592 | bytes 25231360 | tf_op jit(solution)/shard_map/cpkb,pqbm->cqkm/dot_general | solution.py:46
  135.8 2.8 subtract_bitcast_fusion.1
  138.5 4.3 %subtract_bitcast_fusion.2 = (f32[128,64,64]{0,2,1:T(8,128)}, f32[128,64,64]{0,2,1:T(8,128)}, f32[128,64,64]{0,2,1:T(8,128)}, f32[128,64,64]{0,2,1:T(8,128)}) fusion(f32[384,2,64,64]{0,3,2,1:T(8,128)S(1)} %fusion.20), kind=kLoop, calls=%fused_computation.41 | loop fusion | flops 6291456 | bytes 20971520 | tf_op jit(solution)/shard_map/sub | solution.py:92
  142.8 3.7 maximum_bitcast_fusion.1
  148.2 13.8 %fusion.23 = f32[2,64,384,64]{2,1,3,0:T(8,128)} fusion(f32[384,1,64,64]{0,3,2,1:T(8,128)S(1)} %maximum_bitcast_fusion.1, f32[384,1,64,64]{0,3,2,1:T(8,128)S(1)} %maximum_bitcast_fusion, f32[1,2,64,64]{2,3,1,0:T(8,128)S(1)} %get-tuple-element.29, f32[1,2,64,64]{2,3,1,0:T(8,128)S(1)} %get-tuple-element.24), kind=kOutput, calls=%fused_computation.35 | convolution fusion | flops 4835000320 | bytes 25231360 | tf_op jit(solution)/shard_map/cpkm,pqbm->cqkb/dot_general | solution.py:52
  162.0 16.4 %copy.121 = f32[2,64,384,64]{2,3,1,0:T(8,128)} copy(f32[2,64,384,64]{2,1,3,0:T(8,128)} %fusion.23) | data formatting | bytes 25165824 | tf_op jit(solution)/shard_map/cpkm,pqbm->cqkb/dot_general | solution.py:52
  178.4 6.0 %multiply_add_fusion = (f32[384,1,64,64]{0,2,3,1:T(8,128)S(1)}, f32[384,1,64,64]{0,2,3,1:T(8,128)S(1)}) fusion(f32[384,2,64,64]{0,2,3,1:T(8,128)} %bitcast.168, f32[64,64]{0,1:T(8,128)S(1)} %get-tuple-element.36, f32[64,64]{0,1:T(8,128)S(1)} %get-tuple-element.37), kind=kLoop, calls=%fused_computation.30 | loop fusion | flops 9437184 | bytes 25198592 | tf_op jit(solution)/shard_map/add | solution.py:57
  184.3 7.4 %fusion.13 = f32[384,64,64]{0,1,2:T(8,128)S(1)} fusion(f32[384,1,64,64]{0,2,3,1:T(8,128)S(1)} %get-tuple-element.10, f32[384,1,64,64]{0,2,3,1:T(8,128)S(1)} %get-tuple-element.9, f32[1,64,64]{1,2,0:T(8,128)S(1)} %get-tuple-element.34, f32[1,64,64]{1,2,0:T(8,128)S(1)} %get-tuple-element.35), kind=kOutput, calls=%fused_computation.23 | convolution fusion | flops 2420645888 | bytes 18907136 | tf_op jit(solution)/shard_map/cpkb,pak->cab/dot_general | solution.py:62
  191.8 3.6 copy.59
  196.2 1.2 copy-done.4
  197.4 1.1 copy-done.6
  199.8 8.5 %copy.124 = bf16[1,128,2048]{1,0,2:T(2,128)(2,1)S(1)} copy(bf16[1,128,2048]{1,2,0:T(8,128)(2,1)S(1)} %bitcast.182) | data formatting | bytes 1048576 | tf_op jit(solution)/shard_map/reshape | solution.py:147
  208.9 11.5 %reduce.4 = bf16[2048,128]{1,0:T(8,128)(2,1)S(1)} reduce(bf16[2048,1,128]{2,1,0:T(2,128)(2,1)S(1)} %bitcast.174, bf16[]{:T(256)} %broadcast.254), dimensions={1}, to_apply=%bitcast.167.reduce_sub_computation | reduce | bytes 1048578
  221.3 4.0 all-to-all-start.4
  225.4 8.1 %copy.123 = bf16[1,128,2048]{1,0,2:T(2,128)(2,1)S(1)} copy(bf16[1,128,2048]{1,2,0:T(8,128)(2,1)S(1)} %bitcast.181) | data formatting | bytes 1048576 | tf_op jit(solution)/shard_map/reshape | solution.py:147
  233.5 11.5 %reduce.5 = bf16[2048,128]{1,0:T(8,128)(2,1)S(1)} reduce(bf16[2048,1,128]{2,1,0:T(2,128)(2,1)S(1)} %bitcast.176, bf16[]{:T(256)} %broadcast.254), dimensions={1}, to_apply=%bitcast.166.reduce_sub_computation | reduce | bytes 1048578
  246.0 8.3 %copy.122 = bf16[1,128,2048]{1,0,2:T(2,128)(2,1)S(1)} copy(bf16[1,128,2048]{1,2,0:T(8,128)(2,1)S(1)} %bitcast.180) | data formatting | bytes 1048576 | tf_op jit(solution)/shard_map/reshape | solution.py:147
  254.3 11.5 %reduce.6 = bf16[2048,128]{1,0:T(8,128)(2,1)S(1)} reduce(bf16[2048,1,128]{2,1,0:T(2,128)(2,1)S(1)} %bitcast.175, bf16[]{:T(256)} %broadcast.254), dimensions={1}, to_apply=%bitcast.165.reduce_sub_computation | reduce | bytes 1048578
  266.8 7.0 %all-to-all-start.5 = ((bf16[16,2,8192]{2,1,0:T(2,128)(2,1)}), bf16[16,2,8192]{2,1,0:T(2,128)(2,1)S(1)}, u32[]{:S(2)}, u32[]{:S(2)}) async-start(bf16[16,2,8192]{2,1,0:T(2,128)(2,1)} %reshape.265), calls=%async_computation.5 | async-start | bytes 1048576 | tf_op jit(solution)/shard_map/all_to_all | solution.py:167
  273.8 1.6 slice_multiply_fusion
  275.3 2.0 copy.77
  277.6 3.3 multiply_reduce_fusion
  281.0 6.4 %all-to-all-done.5 = bf16[16,2,8192]{2,1,0:T(2,128)(2,1)S(1)} async-done(((bf16[16,2,8192]{2,1,0:T(2,128)(2,1)}), bf16[16,2,8192]{2,1,0:T(2,128)(2,1)S(1)}, u32[]{:S(2)}, u32[]{:S(2)}) %all-to-all-start.5) | async-done | bytes 524320 | tf_op jit(solution)/shard_map/all_to_all | solution.py:167
  287.4 3.8 all-to-all-start.6
  291.2 34.5 %fusion = f32[128,1,16]{2,1,0:T(1,128)S(1)} fusion(f32[128,2048,1]{1,2,0:T(1,128)S(1)} %copy-done.15, f32[2048]{0:T(1024)S(1)} %iota_convert_fusion, f32[128,16]{1,0:T(8,128)S(1)} %copy-done.17), kind=kOutput, calls=%fused_computation.3 | convolution fusion | flops 54525952 | bytes 1073152 | tf_op jit(solution)/shard_map/ct,cmt->cm/dot_general | solution.py:110
  326.3 3.3 all-reduce.2
  329.6 77.1 %all-reduce.1 = (f32[64,16]{0,1:T(8,128)S(1)}, f32[64,16]{0,1:T(8,128)S(1)}) all-reduce(f32[64,16]{0,1:T(8,128)S(1)} %get-tuple-element.7, f32[64,16]{0,1:T(8,128)S(1)} %get-tuple-element.8), channel_id=1, replica_groups=mesh['ctx'=16,'tp'=2] {'ctx'}, use_global_device_ids=true, to_apply=%region_1.2 | all-reduce | flops 2048 | bytes 16384 | tf_op jit(solution)/shard_map/psum | solution.py:9
  408.6 1.0 copy.61
  410.2 1.0 copy.63
  411.9 1.0 copy.65
  (75 shorter events, 14.6 us)
Async XLA Ops:
  0.6 45.7 %copy-start = (f32[64,16]{0,1:T(8,128)S(1)}, f32[64,16]{0,1:T(8,128)}, u32[]{:S(2)}) copy-start(f32[64,16]{0,1:T(8,128)} %param.11) | copy-start | bytes 12292
  24.1 18.4 %all-to-all-start.2 = ((bf16[16,128,128]{2,1,0:T(8,128)(2,1)}), bf16[16,128,128]{2,1,0:T(8,128)(2,1)S(1)}, u32[]{:S(2)}, u32[]{:S(2)}) async-start(bf16[16,128,128]{2,1,0:T(8,128)(2,1)} %bitcast.184), calls=%async_computation.2 | async-start | bytes 1048576 | tf_op jit(solution)/shard_map/all_to_all | solution.py:152
  28.1 37.3 %copy-start.18 = (s32[128]{0:T(128)}, s32[128]{0:T(128)S(1)}, u32[]{:S(2)}) copy-start(s32[128]{0:T(128)S(1)} %and_select_fusion) | copy-start | bytes 1540
  42.5 22.9 %copy-start.13 = (bf16[16,128,128]{2,1,0:T(8,128)(2,1)}, bf16[16,128,128]{2,1,0:T(8,128)(2,1)S(1)}, u32[]{:S(2)}) copy-start(bf16[16,128,128]{2,1,0:T(8,128)(2,1)S(1)} %all-to-all-done.2) | copy-start | bytes 1572868
  42.5 18.3 %all-to-all-start.3 = ((bf16[16,128,128]{2,1,0:T(8,128)(2,1)}), bf16[16,128,128]{2,1,0:T(8,128)(2,1)S(1)}, u32[]{:S(2)}, u32[]{:S(2)}) async-start(bf16[16,128,128]{2,1,0:T(8,128)(2,1)} %bitcast.185), calls=%async_computation.3 | async-start | bytes 1048576 | tf_op jit(solution)/shard_map/all_to_all | solution.py:150
  47.3 18.2 %copy-start.16 = (f32[128,16]{1,0:T(8,128)}, f32[128,16]{1,0:T(8,128)S(1)}, u32[]{:S(2)}) copy-start(f32[128,16]{1,0:T(8,128)S(1)} %copy.49) | copy-start | bytes 24580
  60.8 4.6 %copy-start.14 = (bf16[16,128,128]{2,1,0:T(8,128)(2,1)}, bf16[16,128,128]{2,1,0:T(8,128)(2,1)S(1)}, u32[]{:S(2)}) copy-start(bf16[16,128,128]{2,1,0:T(8,128)(2,1)S(1)} %all-to-all-done.3) | copy-start | bytes 1572868
  60.8 18.4 %all-to-all-start = ((bf16[16,128,128]{2,1,0:T(8,128)(2,1)}), bf16[16,128,128]{2,1,0:T(8,128)(2,1)}, u32[]{:S(2)}, u32[]{:S(2)}) async-start(bf16[16,128,128]{2,1,0:T(8,128)(2,1)} %bitcast.1), calls=%async_computation | async-start | bytes 1048576 | tf_op jit(solution)/shard_map/all_to_all | solution.py:153
  65.8 19.0 %copy-start.3 = (f32[1,128,16,128]{1,3,2,0:T(8,128)}, f32[1,128,16,128]{1,3,2,0:T(8,128)S(1)}, u32[]{:S(2)}) copy-start(f32[1,128,16,128]{1,3,2,0:T(8,128)S(1)} %copy.47) | copy-start | bytes 3145732
  67.7 17.2 %copy-start.5 = (f32[1,128,16,128]{1,3,2,0:T(8,128)}, f32[1,128,16,128]{1,3,2,0:T(8,128)S(1)}, u32[]{:S(2)}) copy-start(f32[1,128,16,128]{1,3,2,0:T(8,128)S(1)} %copy.48) | copy-start | bytes 3145732
  82.8 2.5 copy-start.7
  82.8 2.1 copy-start.12
  142.8 3.7 copy-start.9
  142.8 4.1 copy-start.10
  142.8 4.7 %copy-start.11 = (f32[128,64,64]{0,2,1:T(8,128)S(1)}, f32[128,64,64]{0,2,1:T(8,128)}, u32[]{:S(2)}) copy-start(f32[128,64,64]{0,2,1:T(8,128)} %get-tuple-element.15) | copy-start | bytes 6291460
  195.4 4.4 %copy-start.2 = (f32[384,64,64]{0,2,1:T(8,128)}, f32[384,64,64]{0,2,1:T(8,128)S(1)}, u32[]{:S(2)}) copy-start(f32[384,64,64]{0,2,1:T(8,128)S(1)} %copy.59) | copy-start | bytes 18874372
  195.4 2.0 copy-start.4
  195.4 3.1 copy-start.6
  195.4 4.1 copy-start.8
  221.3 45.4 %all-to-all-start.4 = ((bf16[16,2,8192]{2,1,0:T(2,128)(2,1)}), bf16[16,2,8192]{2,1,0:T(2,128)(2,1)S(1)}, u32[]{:S(2)}, u32[]{:S(2)}) async-start(bf16[16,2,8192]{2,1,0:T(2,128)(2,1)} %reshape.263), calls=%async_computation.4 | async-start | bytes 1048576 | tf_op jit(solution)/shard_map/all_to_all | solution.py:166
  246.0 31.7 %copy-start.17 = (f32[128,16]{1,0:T(8,128)S(1)}, f32[128,16]{1,0:T(8,128)}, u32[]{:S(2)}) copy-start(f32[128,16]{1,0:T(8,128)} %copy-done.16) | copy-start | bytes 24580
  266.8 20.6 %all-to-all-start.5 = ((bf16[16,2,8192]{2,1,0:T(2,128)(2,1)}), bf16[16,2,8192]{2,1,0:T(2,128)(2,1)S(1)}, u32[]{:S(2)}, u32[]{:S(2)}) async-start(bf16[16,2,8192]{2,1,0:T(2,128)(2,1)} %reshape.265), calls=%async_computation.5 | async-start | bytes 1048576 | tf_op jit(solution)/shard_map/all_to_all | solution.py:167
  277.6 13.6 %copy-start.15 = (f32[128,2048,1]{1,2,0:T(1,128)S(1)}, f32[128,2048,1]{1,2,0:T(1,128)}, u32[]{:S(2)}) copy-start(f32[128,2048,1]{1,2,0:T(1,128)} %copy.77) | copy-start | bytes 3145732
  287.4 123.9 %all-to-all-start.6 = ((bf16[16,2,8192]{2,1,0:T(2,128)(2,1)}), bf16[16,2,8192]{2,1,0:T(2,128)(2,1)S(1)}, u32[]{:S(2)}, u32[]{:S(2)}) async-start(bf16[16,2,8192]{2,1,0:T(2,128)(2,1)} %reshape.267), calls=%async_computation.6 | async-start | bytes 1048576 | tf_op jit(solution)/shard_map/all_to_all | solution.py:168
  291.2 34.6 %copy-start.19 = (s32[128]{0:T(128)S(1)}, s32[128]{0:T(128)}, u32[]{:S(2)}) copy-start(s32[128]{0:T(128)} %copy-done.18) | copy-start | bytes 1540
  291.2 34.6 %copy-start.20 = (f32[128,16]{0,1:T(8,128)S(1)}, f32[128,16]{0,1:T(8,128)}, u32[]{:S(2)}) copy-start(f32[128,16]{0,1:T(8,128)} %get-tuple-element.31) | copy-start | bytes 24580
  407.4 5.5 %copy-start.1 = (f32[64,16]{0,1:T(8,128)S(1)}, f32[64,16]{0,1:T(8,128)}, u32[]{:S(2)}) copy-start(f32[64,16]{0,1:T(8,128)} %param.11) | copy-start | bytes 12292
